TPU v7x, 256 devices: a whole 4x4x8 slice. The times are simulated.
256 devices in a mesh: dp: 32 (over y_lo, z, core), tensor: 8 (over y_hi, x).
Axes of the slice: x: 4, y: 4 (y_hi: 2, y_lo: 2; y = y_hi * 2 + y_lo), z: 8, core: 2. Of those that a mesh axis runs over, the one named last changes fastest.
Arguments:
- activations: bfloat16 [1024, 16384], P('dp', 'tensor'), may hold values from -6 to 6
- weight: bfloat16 [16384, 16384], P('tensor', 'dp'), may hold values from -0.046875 to 0.046875
- out_grad: bfloat16 [1024, 16384], P('tensor', 'dp'), may hold values from -6 to 6
Outputs:
- outputs: bfloat16 [1024, 16384], P('tensor', 'dp')
- in_grad: bfloat16 [1024, 16384], P('dp', 'tensor')
- weight_grad: float32 [16384, 16384], P('tensor', 'dp')
All inputs are finite; a program needn't handle non-finite values.
Results may differ from a plain program's by a relative error of at most 0.0049.
Values may be sent and summed in bfloat16 or wider, within the bound.
A program may use at most 64 MiB of HBM per device.

v0:
```python
import math
import jax
import jax.numpy as jnp
from jax import lax
from jax.sharding import PartitionSpec as P


def from_partner(shard, axis, apart):
    return lax.ppermute(shard, axis, [(i, i ^ 1 << apart) for i in range(lax.axis_size(axis))])


def signs_table(width):
    position = jnp.arange(width, dtype=jnp.int32)
    joined = jnp.bitwise_and(position[:, None], position[None, :])
    parity = jnp.zeros_like(joined)
    for bit_number in range(width.bit_length() - 1):
        parity = parity + jnp.bitwise_and(jnp.right_shift(joined, bit_number), 1)
    return jnp.where(parity % 2 == 1, -1.0, 1.0).astype(jnp.float32)


def transform(values, width):
    bit_count = width.bit_length() - 1
    first_size = 2 ** (bit_count // 2)
    second = width // first_size
    shaped = values.reshape(values.shape[0], first_size, second)
    result = jnp.einsum(
        "rab,ac->rcb", shaped, signs_table(first_size), precision=lax.Precision.HIGHEST
    )
    result = jnp.einsum("rcb,bd->rcd", result, signs_table(second), precision=lax.Precision.HIGHEST)
    return result.reshape(values.shape[0], width)


def rotate_pairs(values, width):
    result = transform(values, width)
    position = lax.axis_index("tensor")
    for bit_number in range(lax.axis_size("tensor").bit_length() - 1):
        other = from_partner(result, "tensor", bit_number)
        upper = jnp.bitwise_and(jnp.right_shift(position, bit_number), 1) == 1
        result = jnp.where(upper, other - result, result + other)
    return result


def per_device(activations, weight, out_grad):
    tensor_size = lax.axis_size("tensor")
    local_width = activations.shape[1]
    full_width = local_width * tensor_size
    factor = 1.0 / math.sqrt(full_width)
    grad_count = out_grad.shape[0]
    token_total = grad_count * tensor_size
    rotated = (rotate_pairs(activations.astype(jnp.float32), local_width) * factor).astype(
        jnp.bfloat16
    )
    grad_all = lax.all_gather(out_grad, "tensor", axis=0, tiled=True)
    rows_all = lax.all_gather(rotated, "dp", axis=0, tiled=True)
    weight_grad = lax.dot_general(
        rows_all, grad_all, (((0,), (0,)), ((), ())), preferred_element_type=jnp.float32
    )
    outputs = lax.psum_scatter(
        jnp.dot(rows_all, weight, preferred_element_type=jnp.float32),
        "tensor",
        scatter_dimension=0,
        tiled=True,
    ).astype(jnp.bfloat16)
    weight_grad = weight_grad * (1.0 / math.sqrt(token_total))
    rotated_grad = lax.psum_scatter(
        lax.dot_general(
            grad_all, weight, (((1,), (1,)), ((), ())), preferred_element_type=jnp.float32
        ),
        "dp",
        scatter_dimension=0,
        tiled=True,
    )
    in_grad = (rotate_pairs(rotated_grad, local_width) * factor).astype(jnp.bfloat16)
    return (outputs, in_grad, weight_grad)


def solution(mesh):
    return jax.shard_map(
        per_device,
        mesh=mesh,
        in_specs=(P("dp", "tensor"), P("tensor", "dp"), P("tensor", "dp")),
        out_specs=(P("tensor", "dp"), P("dp", "tensor"), P("tensor", "dp")),
        check_vma=False,
    )
```

profile of v0, /device:TPU:2, one launch (start us, length us, event | category | flops | bytes accessed | tf_op | source)
XLA Modules:
  0.0 356.3 jit_solution(6116350609848868271)
XLA Ops:
  7.2 0.0 copy-start
  7.2 0.0 all-gather.5.cloned.1.call-start
  7.2 1.3 reshape.18
  8.5 0.4 convolution_bitcast_fusion.1
  9.0 0.6 fusion.4
  9.6 0.2 reshape.19
  9.8 2.3 collective-permute-start
  12.1 0.0 all-gather.5.cloned.1.call-update
  12.2 0.0 all-gather.3.cloned.1.call-start
  12.2 5.7 %collective-permute-done = f32[32,2048]{1,0:T(8,128)S(1)} collective-permute-done((f32[32,2048]{1,0:T(8,128)S(1)}, f32[32,2048]{1,0:T(8,128)S(1)}, u32[]{:S(2)}, u32[]{:S(2)}) %collective-permute-start) | collective-permute-done | bytes 262176 | tf_op jit(solution)/shard_map/ppermute | solution.py:9
  17.9 2.2 collective-permute-start.1
  20.1 6.3 %collective-permute-done.1 = f32[32,2048]{1,0:T(8,128)S(1)} collective-permute-done((f32[32,2048]{1,0:T(8,128)S(1)}, f32[32,2048]{1,0:T(8,128)S(1)}, u32[]{:S(2)}, u32[]{:S(2)}) %collective-permute-start.1) | collective-permute-done | bytes 262176 | tf_op jit(solution)/shard_map/ppermute | solution.py:9
  26.4 3.6 %collective-permute-start.2 = (f32[32,2048]{1,0:T(8,128)S(1)}, f32[32,2048]{1,0:T(8,128)S(1)}, u32[]{:S(2)}, u32[]{:S(2)}) collective-permute-start(f32[32,2048]{1,0:T(8,128)S(1)} %add_select_fusion.2), channel_id=1, source_target_pairs={{0,4},{1,5},{2,6},{3,7},{4,0},{5,1},{6,2},{7,3},{8,12},{9,13},{10,... | collective-permute-start | bytes 786440 | tf_op jit(solution)/shard_map/ppermute | solution.py:9
  30.0 5.9 %collective-permute-done.2 = f32[32,2048]{1,0:T(8,128)S(1)} collective-permute-done((f32[32,2048]{1,0:T(8,128)S(1)}, f32[32,2048]{1,0:T(8,128)S(1)}, u32[]{:S(2)}, u32[]{:S(2)}) %collective-permute-start.2) | collective-permute-done | bytes 262176 | tf_op jit(solution)/shard_map/ppermute | solution.py:9
  35.9 0.7 multiply_convert_fusion.1
  36.6 0.0 all-gather.3.cloned.1.call-update
  36.6 0.0 reduce-scatter.5.cloned.1.call-start
  36.7 29.8 %all-gather.5.cloned.1.call-done = bf16[1024,512]{1,0:T(8,128)(2,1)} async-done(((bf16[128,512]{1,0:T(8,128)(2,1)}), bf16[1024,512]{1,0:T(8,128)(2,1)}) %all-gather.5.cloned.1.call-update) | async-done | bytes 1048592 | tf_op jit(solution)/shard_map/all_gather | solution.py:53
  66.4 0.0 copy-done
  66.4 6.8 %fusion.57 = f32[1024,2048]{1,0:T(8,128)} fusion(bf16[1024,512]{1,0:T(8,128)(2,1)} %all-gather.5.cloned.1.call-done, bf16[2048,512]{1,0:T(8,128)(2,1)S(1)} %copy-done), kind=kOutput, calls=%fused_computation.68 | convolution fusion | flops 2147483648 | bytes 11534336 | tf_op jit(solution)/shard_map/dot_general | solution.py:66
  73.3 0.0 reduce-scatter.5.cloned.1.call-update
  73.3 0.0 reduce-scatter.3.cloned.1.call-start
  73.3 61.5 %all-gather.3.cloned.1.call-done = bf16[1024,2048]{1,0:T(8,128)(2,1)} async-done(((bf16[32,2048]{1,0:T(8,128)(2,1)}), bf16[1024,2048]{1,0:T(8,128)(2,1)}) %all-gather.3.cloned.1.call-update) | async-done | bytes 4194320 | tf_op jit(solution)/shard_map/all_gather | solution.py:54
  134.9 5.8 %fusion.56 = f32[1024,512]{1,0:T(8,128)} fusion(bf16[1024,2048]{1,0:T(8,128)(2,1)} %all-gather.3.cloned.1.call-done, bf16[2048,512]{1,0:T(8,128)(2,1)S(1)} %copy-done), kind=kOutput, calls=%fused_computation.67 | convolution fusion | flops 2147483648 | bytes 8388608 | tf_op jit(solution)/shard_map/dot_general | solution.py:59
  140.7 0.0 reduce-scatter.3.cloned.1.call-update
  140.7 125.6 %reduce-scatter.5.cloned.1.call-done = f32[32,2048]{1,0:T(8,128)} async-done(((f32[1024,2048]{1,0:T(8,128)}), f32[32,2048]{1,0:T(8,128)}) %reduce-scatter.5.cloned.1.call-update) | async-done | bytes 262160 | tf_op jit(solution)/shard_map/reduce_scatter | solution.py:65
  266.4 1.1 reshape.20
  267.5 0.6 convolution_bitcast_fusion
  268.2 0.6 fusion.2
  268.8 0.2 reshape.21
  268.9 0.2 collective-permute-start.3
  269.2 7.7 %collective-permute-done.3 = f32[32,2048]{1,0:T(8,128)S(1)} collective-permute-done((f32[32,2048]{1,0:T(8,128)S(1)}, f32[32,2048]{1,0:T(8,128)S(1)}, u32[]{:S(2)}, u32[]{:S(2)}) %collective-permute-start.3) | collective-permute-done | bytes 262176 | tf_op jit(solution)/shard_map/ppermute | solution.py:9
  276.9 2.9 collective-permute-start.4
  279.7 5.2 %collective-permute-done.4 = f32[32,2048]{1,0:T(8,128)S(1)} collective-permute-done((f32[32,2048]{1,0:T(8,128)S(1)}, f32[32,2048]{1,0:T(8,128)S(1)}, u32[]{:S(2)}, u32[]{:S(2)}) %collective-permute-start.4) | collective-permute-done | bytes 262176 | tf_op jit(solution)/shard_map/ppermute | solution.py:9
  284.9 4.0 %collective-permute-start.5 = (f32[32,2048]{1,0:T(8,128)S(1)}, f32[32,2048]{1,0:T(8,128)S(1)}, u32[]{:S(2)}, u32[]{:S(2)}) collective-permute-start(f32[32,2048]{1,0:T(8,128)S(1)} %add_select_fusion), channel_id=1, source_target_pairs={{0,4},{1,5},{2,6},{3,7},{4,0},{5,1},{6,2},{7,3},{8,12},{9,13},{10,... | collective-permute-start | bytes 786440 | tf_op jit(solution)/shard_map/ppermute | solution.py:9
  289.0 6.9 %convolution_multiply_fusion = f32[2048,512]{1,0:T(8,128)} fusion(bf16[1024,2048]{1,0:T(8,128)(2,1)} %all-gather.3.cloned.1.call-done, bf16[1024,512]{1,0:T(8,128)(2,1)} %all-gather.5.cloned.1.call-done), kind=kOutput, calls=%fused_computation | convolution fusion | flops 2148532224 | bytes 9437184 | tf_op jit(solution)/shard_map/dot_general | solution.py:55
  295.9 51.6 %reduce-scatter.3.cloned.1.call-done = f32[128,512]{1,0:T(8,128)} async-done(((f32[1024,512]{1,0:T(8,128)}), f32[128,512]{1,0:T(8,128)}) %reduce-scatter.3.cloned.1.call-update) | async-done | bytes 262160 | tf_op jit(solution)/shard_map/reduce_scatter | solution.py:58
  347.5 1.6 convert_element_type.11
  349.1 0.0 collective-permute-done.5
  349.1 0.7 multiply_convert_fusion
  (4 shorter events, 0.1 us)
Async XLA Ops:
  7.2 59.3 %copy-start = (bf16[2048,512]{1,0:T(8,128)(2,1)S(1)}, bf16[2048,512]{1,0:T(8,128)(2,1)}, u32[]{:S(2)}) copy-start(bf16[2048,512]{1,0:T(8,128)(2,1)} %param.4) | copy-start | bytes 6291460
  7.2 59.3 %all-gather.5.cloned.1.call-start = ((), (), s32[]{:S(2)}) async-start(), calls=%async_computation.4 | async-start | bytes 1179648 | tf_op jit(solution)/shard_map/all_gather | solution.py:53
  9.8 8.1 %collective-permute-start = (f32[32,2048]{1,0:T(8,128)S(1)}, f32[32,2048]{1,0:T(8,128)S(1)}, u32[]{:S(2)}, u32[]{:S(2)}) collective-permute-start(f32[32,2048]{1,0:T(8,128)S(1)} %reshape.19), channel_id=1, source_target_pairs={{0,1},{1,0},{2,3},{3,2},{4,5},{5,4},{6,7},{7,6},{8,9},{9,8},{10,11... | collective-permute-start | bytes 786440 | tf_op jit(solution)/shard_map/ppermute | solution.py:9
  12.2 122.7 %all-gather.3.cloned.1.call-start = ((), (), s32[]{:S(2)}) async-start(), calls=%async_computation.2 | async-start | bytes 4325376 | tf_op jit(solution)/shard_map/all_gather | solution.py:54
  17.9 8.5 %collective-permute-start.1 = (f32[32,2048]{1,0:T(8,128)S(1)}, f32[32,2048]{1,0:T(8,128)S(1)}, u32[]{:S(2)}, u32[]{:S(2)}) collective-permute-start(f32[32,2048]{1,0:T(8,128)S(1)} %add_select_fusion.3), channel_id=1, source_target_pairs={{0,2},{1,3},{2,0},{3,1},{4,6},{5,7},{6,4},{7,5},{8,10},{9,11},{10,... | collective-permute-start | bytes 786440 | tf_op jit(solution)/shard_map/ppermute | solution.py:9
  26.4 9.5 %collective-permute-start.2 = (f32[32,2048]{1,0:T(8,128)S(1)}, f32[32,2048]{1,0:T(8,128)S(1)}, u32[]{:S(2)}, u32[]{:S(2)}) collective-permute-start(f32[32,2048]{1,0:T(8,128)S(1)} %add_select_fusion.2), channel_id=1, source_target_pairs={{0,4},{1,5},{2,6},{3,7},{4,0},{5,1},{6,2},{7,3},{8,12},{9,13},{10,... | collective-permute-start | bytes 786440 | tf_op jit(solution)/shard_map/ppermute | solution.py:9
  36.6 229.7 %reduce-scatter.5.cloned.1.call-start = ((), (), s32[]{:S(2)}) async-start(), calls=%async_computation.5 | async-start | bytes 8650752 | tf_op jit(solution)/shard_map/reduce_scatter | solution.py:65
  73.3 274.2 %reduce-scatter.3.cloned.1.call-start = ((), (), s32[]{:S(2)}) async-start(), calls=%async_computation.3 | async-start | bytes 2359296 | tf_op jit(solution)/shard_map/reduce_scatter | solution.py:58
  268.9 7.9 %collective-permute-start.3 = (f32[32,2048]{1,0:T(8,128)S(1)}, f32[32,2048]{1,0:T(8,128)S(1)}, u32[]{:S(2)}, u32[]{:S(2)}) collective-permute-start(f32[32,2048]{1,0:T(8,128)S(1)} %reshape.21), channel_id=1, source_target_pairs={{0,1},{1,0},{2,3},{3,2},{4,5},{5,4},{6,7},{7,6},{8,9},{9,8},{10,11... | collective-permute-start | bytes 786440 | tf_op jit(solution)/shard_map/ppermute | solution.py:9
  276.9 8.0 %collective-permute-start.4 = (f32[32,2048]{1,0:T(8,128)S(1)}, f32[32,2048]{1,0:T(8,128)S(1)}, u32[]{:S(2)}, u32[]{:S(2)}) collective-permute-start(f32[32,2048]{1,0:T(8,128)S(1)} %add_select_fusion.1), channel_id=1, source_target_pairs={{0,2},{1,3},{2,0},{3,1},{4,6},{5,7},{6,4},{7,5},{8,10},{9,11},{10,... | collective-permute-start | bytes 786440 | tf_op jit(solution)/shard_map/ppermute | solution.py:9
  284.9 64.2 %collective-permute-start.5 = (f32[32,2048]{1,0:T(8,128)S(1)}, f32[32,2048]{1,0:T(8,128)S(1)}, u32[]{:S(2)}, u32[]{:S(2)}) collective-permute-start(f32[32,2048]{1,0:T(8,128)S(1)} %add_select_fusion), channel_id=1, source_target_pairs={{0,4},{1,5},{2,6},{3,7},{4,0},{5,1},{6,2},{7,3},{8,12},{9,13},{10,... | collective-permute-start | bytes 786440 | tf_op jit(solution)/shard_map/ppermute | solution.py:9
Sparse Core Ops, SparseCore 0:
  12.3 54.1 all-gather.4
  68.9 65.9 all-gather.2
  137.4 128.8 reduce-scatter.4
  270.3 77.1 reduce-scatter.2
where the time goes:
time: 357 us; the launch traced here: 356 us
  waiting for transfers between devices  299 us (84%)
  matrix products  21.9 us (6%)
  starting transfers between devices  15.4 us (4%)
  between operations  13.8 us (4%)
    reduce_scatter x1, waiting for transfers between devices, per_device(): lax.psum_scatter(lax.dot_general(grad_all, weight, (((1,), (1,)), ((), ()...  126 us
    all_gather x1, waiting for transfers between devices, per_device(): rows_all = lax.all_gather(rotated, 'dp', axis=0, tiled=True)  61.5 us
    reduce_scatter x1, waiting for transfers between devices, per_device(): lax.psum_scatter(jnp.dot(rows_all, weight, preferred_element_type=jnp.flo...  51.6 us
    ppermute x6, waiting for transfers between devices, from_partner(): lax.ppermute(shard, axis, [(i, i ^ 1 << apart) for i in range(lax.axis_si...  30.7 us
    all_gather x1, waiting for transfers between devices, per_device(): grad_all = lax.all_gather(out_grad, 'tensor', axis=0, tiled=True)  29.8 us
    ppermute x6, starting transfers between devices, from_partner(): lax.ppermute(shard, axis, [(i, i ^ 1 << apart) for i in range(lax.axis_si...  15.2 us
  transfers between devices with their start and end apart: 10, of which 9 were waited for; matrix products, arithmetic and copies ran while one was open for 7% of the time, Pallas kernels for 0%

commit v1 on v0

--- a/solution.py
+++ b/solution.py
@@ -50,7 +50,15 @@
     rotated = (rotate_pairs(activations.astype(jnp.float32), local_width) * factor).astype(
         jnp.bfloat16
     )
-    grad_all = lax.all_gather(out_grad, "tensor", axis=0, tiled=True)
+    grad_all = jnp.concatenate(
+        lax.all_to_all(
+            jnp.stack([out_grad] * lax.psum(1, axis_name="tensor")),
+            axis_name="tensor",
+            split_axis=0,
+            concat_axis=0,
+        ),
+        axis=0,
+    )
     rows_all = lax.all_gather(rotated, "dp", axis=0, tiled=True)
     weight_grad = lax.dot_general(
         rows_all, grad_all, (((0,), (0,)), ((), ())), preferred_element_type=jnp.float32

time: 357 us -> 328 us (0.919)
  waiting for transfers between devices: 299 us -> 248 us
  blocking collectives: 0 us -> 20.7 us
    all_gather x1 -> x0, waiting for transfers between devices: 29.8 us -> none  [per_device(): grad_all = lax.all_gather(out_grad, 'tensor', axis=0, tiled=True)]
    all_to_all x0 -> x1, blocking collectives: none -> 20.7 us  [per_device(): lax.all_to_all(jnp.stack([out_grad] * lax.psum(1, axis_name='tensor')), a...]
    all_gather x1, waiting for transfers between devices: 61.5 us -> 42.9 us  [per_device(): rows_all = lax.all_gather(rotated, 'dp', axis=0, tiled=True)]
  transfers between devices with their start and end apart: 10 -> 9, of which waited for: 9 -> 8; matrix products, arithmetic and copies ran while one was open for 7% -> 7% of each run, Pallas kernels for 0% -> 0%
where the time goes in v1:
time: 328 us
  waiting for transfers between devices  248 us (76%)
  blocking collectives  20.7 us (6%)
  matrix products  20.6 us (6%)
  starting transfers between devices  17.1 us (5%)
  between operations  13.8 us (4%)
  local copies, waits for them, and re-layouts  3.93 us (1%)
    reduce_scatter x1, waiting for transfers between devices, per_device(): lax.psum_scatter(lax.dot_general(grad_all, weight, (((1,), (1,)), ((), ()...  126 us
    reduce_scatter x1, waiting for transfers between devices, per_device(): lax.psum_scatter(jnp.dot(rows_all, weight, preferred_element_type=jnp.flo...  51.8 us
    all_gather x1, waiting for transfers between devices, per_device(): rows_all = lax.all_gather(rotated, 'dp', axis=0, tiled=True)  42.9 us
    ppermute x6, waiting for transfers between devices, from_partner(): lax.ppermute(shard, axis, [(i, i ^ 1 << apart) for i in range(lax.axis_si...  27.9 us
    all_to_all x1, blocking collectives, per_device(): lax.all_to_all(jnp.stack([out_grad] * lax.psum(1, axis_name='tensor')), a...  20.7 us
    ppermute x6, starting transfers between devices, from_partner(): lax.ppermute(shard, axis, [(i, i ^ 1 << apart) for i in range(lax.axis_si...  17 us
    dot_general x1, matrix products, per_device(): lax.dot_general(rows_all, grad_all, (((0,), (0,)), ((), ())), preferred_e...  6.96 us
  transfers between devices with their start and end apart: 9, of which 8 were waited for; matrix products, arithmetic and copies ran while one was open for 7% of the time, Pallas kernels for 0%

profile of v1, /device:TPU:2, one launch (start us, length us, event | category | flops | bytes accessed | tf_op | source)
XLA Modules:
  0.0 327.6 jit_solution(3059029615582599693)
XLA Ops:
  7.2 0.0 copy-start
  7.2 0.0 copy-start.2
  7.2 0.0 all-gather.2.cloned.1.call-start
  7.2 1.3 reshape.23
  8.6 0.4 convolution_bitcast_fusion.1
  9.0 0.6 fusion.4
  9.6 0.2 reshape.24
  9.8 2.4 collective-permute-start
  12.2 5.8 %collective-permute-done = f32[32,2048]{1,0:T(8,128)S(1)} collective-permute-done((f32[32,2048]{1,0:T(8,128)S(1)}, f32[32,2048]{1,0:T(8,128)S(1)}, u32[]{:S(2)}, u32[]{:S(2)}) %collective-permute-start) | collective-permute-done | bytes 262176 | tf_op jit(solution)/shard_map/ppermute | solution.py:9
  18.0 2.2 collective-permute-start.1
  20.2 6.3 %collective-permute-done.1 = f32[32,2048]{1,0:T(8,128)S(1)} collective-permute-done((f32[32,2048]{1,0:T(8,128)S(1)}, f32[32,2048]{1,0:T(8,128)S(1)}, u32[]{:S(2)}, u32[]{:S(2)}) %collective-permute-start.1) | collective-permute-done | bytes 262176 | tf_op jit(solution)/shard_map/ppermute | solution.py:9
  26.5 3.6 %collective-permute-start.2 = (f32[32,2048]{1,0:T(8,128)S(1)}, f32[32,2048]{1,0:T(8,128)S(1)}, u32[]{:S(2)}, u32[]{:S(2)}) collective-permute-start(f32[32,2048]{1,0:T(8,128)S(1)} %add_select_fusion.2), channel_id=1, source_target_pairs={{0,4},{1,5},{2,6},{3,7},{4,0},{5,1},{6,2},{7,3},{8,12},{9,13},{10,... | collective-permute-start | bytes 786440 | tf_op jit(solution)/shard_map/ppermute | solution.py:9
  30.0 4.5 %collective-permute-done.2 = f32[32,2048]{1,0:T(8,128)S(1)} collective-permute-done((f32[32,2048]{1,0:T(8,128)S(1)}, f32[32,2048]{1,0:T(8,128)S(1)}, u32[]{:S(2)}, u32[]{:S(2)}) %collective-permute-start.2) | collective-permute-done | bytes 262176 | tf_op jit(solution)/shard_map/ppermute | solution.py:9
  34.6 0.7 multiply_convert_fusion.1
  35.3 0.0 all-gather.2.cloned.1.call-update
  35.3 0.0 reduce-scatter.5.cloned.1.call-start
  35.3 0.0 copy-done.2
  35.3 0.1 stack.2
  35.4 20.7 %all_to_all.5 = bf16[8,128,512]{2,1,0:T(8,128)(2,1)S(1)} all-to-all(bf16[8,128,512]{2,1,0:T(8,128)(2,1)S(1)} %stack.2), channel_id=1, replica_groups=mesh['dp'=32,'tensor'=8] {'tensor'}, dimensions={0} | all-to-all | bytes 2097152 | tf_op jit(solution)/shard_map/all_to_all | solution.py:54
  56.1 0.0 copy-start.1
  56.1 1.0 copy-done.1
  57.1 0.0 copy-done
  57.1 5.6 %fusion.57 = f32[1024,2048]{1,0:T(8,128)} fusion(bf16[1024,512]{1,0:T(8,128)(2,1)S(1)} %bitcast.25, bf16[2048,512]{1,0:T(8,128)(2,1)S(1)} %copy-done), kind=kOutput, calls=%fused_computation.68 | convolution fusion | flops 2147483648 | bytes 11534336 | tf_op jit(solution)/shard_map/dot_general | solution.py:74
  62.7 0.0 reduce-scatter.5.cloned.1.call-update
  62.7 0.0 reduce-scatter.3.cloned.1.call-start
  62.8 42.9 %all-gather.2.cloned.1.call-done = bf16[1024,2048]{1,0:T(8,128)(2,1)} async-done(((bf16[32,2048]{1,0:T(8,128)(2,1)}), bf16[1024,2048]{1,0:T(8,128)(2,1)}) %all-gather.2.cloned.1.call-update) | async-done | bytes 4194320 | tf_op jit(solution)/shard_map/all_gather | solution.py:62
  105.6 5.8 %fusion.56 = f32[1024,512]{1,0:T(8,128)} fusion(bf16[1024,2048]{1,0:T(8,128)(2,1)} %all-gather.2.cloned.1.call-done, bf16[2048,512]{1,0:T(8,128)(2,1)S(1)} %copy-done), kind=kOutput, calls=%fused_computation.67 | convolution fusion | flops 2147483648 | bytes 8388608 | tf_op jit(solution)/shard_map/dot_general | solution.py:67
  111.4 0.0 reduce-scatter.3.cloned.1.call-update
  111.5 125.6 %reduce-scatter.5.cloned.1.call-done = f32[32,2048]{1,0:T(8,128)} async-done(((f32[1024,2048]{1,0:T(8,128)}), f32[32,2048]{1,0:T(8,128)}) %reduce-scatter.5.cloned.1.call-update) | async-done | bytes 262160 | tf_op jit(solution)/shard_map/reduce_scatter | solution.py:73
  237.1 1.1 reshape.26
  238.3 0.6 convolution_bitcast_fusion
  238.9 0.6 fusion.2
  239.5 0.2 reshape.27
  239.7 1.0 collective-permute-start.3
  240.7 6.5 %collective-permute-done.3 = f32[32,2048]{1,0:T(8,128)S(1)} collective-permute-done((f32[32,2048]{1,0:T(8,128)S(1)}, f32[32,2048]{1,0:T(8,128)S(1)}, u32[]{:S(2)}, u32[]{:S(2)}) %collective-permute-start.3) | collective-permute-done | bytes 262176 | tf_op jit(solution)/shard_map/ppermute | solution.py:9
  247.2 3.9 %collective-permute-start.4 = (f32[32,2048]{1,0:T(8,128)S(1)}, f32[32,2048]{1,0:T(8,128)S(1)}, u32[]{:S(2)}, u32[]{:S(2)}) collective-permute-start(f32[32,2048]{1,0:T(8,128)S(1)} %add_select_fusion.1), channel_id=1, source_target_pairs={{0,2},{1,3},{2,0},{3,1},{4,6},{5,7},{6,4},{7,5},{8,10},{9,11},{10,... | collective-permute-start | bytes 786440 | tf_op jit(solution)/shard_map/ppermute | solution.py:9
  251.1 4.8 %collective-permute-done.4 = f32[32,2048]{1,0:T(8,128)S(1)} collective-permute-done((f32[32,2048]{1,0:T(8,128)S(1)}, f32[32,2048]{1,0:T(8,128)S(1)}, u32[]{:S(2)}, u32[]{:S(2)}) %collective-permute-start.4) | collective-permute-done | bytes 262176 | tf_op jit(solution)/shard_map/ppermute | solution.py:9
  256.0 4.0 %collective-permute-start.5 = (f32[32,2048]{1,0:T(8,128)S(1)}, f32[32,2048]{1,0:T(8,128)S(1)}, u32[]{:S(2)}, u32[]{:S(2)}) collective-permute-start(f32[32,2048]{1,0:T(8,128)S(1)} %add_select_fusion), channel_id=1, source_target_pairs={{0,4},{1,5},{2,6},{3,7},{4,0},{5,1},{6,2},{7,3},{8,12},{9,13},{10,... | collective-permute-start | bytes 786440 | tf_op jit(solution)/shard_map/ppermute | solution.py:9
  260.0 7.0 %convolution_multiply_fusion = f32[2048,512]{1,0:T(8,128)} fusion(bf16[1024,2048]{1,0:T(8,128)(2,1)} %all-gather.2.cloned.1.call-done, bf16[1024,512]{1,0:T(8,128)(2,1)} %bitcast.26), kind=kOutput, calls=%fused_computation | convolution fusion | flops 2148532224 | bytes 9437184 | tf_op jit(solution)/shard_map/dot_general | solution.py:63
  266.9 51.8 %reduce-scatter.3.cloned.1.call-done = f32[128,512]{1,0:T(8,128)} async-done(((f32[1024,512]{1,0:T(8,128)}), f32[128,512]{1,0:T(8,128)}) %reduce-scatter.3.cloned.1.call-update) | async-done | bytes 262160 | tf_op jit(solution)/shard_map/reduce_scatter | solution.py:66
  318.7 1.6 convert_element_type.11
  320.4 0.0 collective-permute-done.5
  320.4 0.7 multiply_convert_fusion
  (4 shorter events, 0.1 us)
Async XLA Ops:
  7.2 49.9 %copy-start = (bf16[2048,512]{1,0:T(8,128)(2,1)S(1)}, bf16[2048,512]{1,0:T(8,128)(2,1)}, u32[]{:S(2)}) copy-start(bf16[2048,512]{1,0:T(8,128)(2,1)} %param.4) | copy-start | bytes 6291460
  7.2 28.1 %copy-start.2 = (bf16[128,512]{1,0:T(8,128)(2,1)S(1)}, bf16[128,512]{1,0:T(8,128)(2,1)}, u32[]{:S(2)}) copy-start(bf16[128,512]{1,0:T(8,128)(2,1)} %param.5) | copy-start | bytes 393220
  7.2 98.4 %all-gather.2.cloned.1.call-start = ((), (), s32[]{:S(2)}) async-start(), calls=%async_computation.3 | async-start | bytes 4325376 | tf_op jit(solution)/shard_map/all_gather | solution.py:62
  9.8 8.1 %collective-permute-start = (f32[32,2048]{1,0:T(8,128)S(1)}, f32[32,2048]{1,0:T(8,128)S(1)}, u32[]{:S(2)}, u32[]{:S(2)}) collective-permute-start(f32[32,2048]{1,0:T(8,128)S(1)} %reshape.24), channel_id=1, source_target_pairs={{0,1},{1,0},{2,3},{3,2},{4,5},{5,4},{6,7},{7,6},{8,9},{9,8},{10,11... | collective-permute-start | bytes 786440 | tf_op jit(solution)/shard_map/ppermute | solution.py:9
  18.0 8.5 %collective-permute-start.1 = (f32[32,2048]{1,0:T(8,128)S(1)}, f32[32,2048]{1,0:T(8,128)S(1)}, u32[]{:S(2)}, u32[]{:S(2)}) collective-permute-start(f32[32,2048]{1,0:T(8,128)S(1)} %add_select_fusion.3), channel_id=1, source_target_pairs={{0,2},{1,3},{2,0},{3,1},{4,6},{5,7},{6,4},{7,5},{8,10},{9,11},{10,... | collective-permute-start | bytes 786440 | tf_op jit(solution)/shard_map/ppermute | solution.py:9
  26.5 8.1 %collective-permute-start.2 = (f32[32,2048]{1,0:T(8,128)S(1)}, f32[32,2048]{1,0:T(8,128)S(1)}, u32[]{:S(2)}, u32[]{:S(2)}) collective-permute-start(f32[32,2048]{1,0:T(8,128)S(1)} %add_select_fusion.2), channel_id=1, source_target_pairs={{0,4},{1,5},{2,6},{3,7},{4,0},{5,1},{6,2},{7,3},{8,12},{9,13},{10,... | collective-permute-start | bytes 786440 | tf_op jit(solution)/shard_map/ppermute | solution.py:9
  35.3 201.8 %reduce-scatter.5.cloned.1.call-start = ((), (), s32[]{:S(2)}) async-start(), calls=%async_computation.5 | async-start | bytes 8650752 | tf_op jit(solution)/shard_map/reduce_scatter | solution.py:73
  56.1 1.0 copy-start.1
  62.7 256.0 %reduce-scatter.3.cloned.1.call-start = ((), (), s32[]{:S(2)}) async-start(), calls=%async_computation.4 | async-start | bytes 2359296 | tf_op jit(solution)/shard_map/reduce_scatter | solution.py:66
  239.7 7.5 %collective-permute-start.3 = (f32[32,2048]{1,0:T(8,128)S(1)}, f32[32,2048]{1,0:T(8,128)S(1)}, u32[]{:S(2)}, u32[]{:S(2)}) collective-permute-start(f32[32,2048]{1,0:T(8,128)S(1)} %reshape.27), channel_id=1, source_target_pairs={{0,1},{1,0},{2,3},{3,2},{4,5},{5,4},{6,7},{7,6},{8,9},{9,8},{10,11... | collective-permute-start | bytes 786440 | tf_op jit(solution)/shard_map/ppermute | solution.py:9
  247.2 8.7 %collective-permute-start.4 = (f32[32,2048]{1,0:T(8,128)S(1)}, f32[32,2048]{1,0:T(8,128)S(1)}, u32[]{:S(2)}, u32[]{:S(2)}) collective-permute-start(f32[32,2048]{1,0:T(8,128)S(1)} %add_select_fusion.1), channel_id=1, source_target_pairs={{0,2},{1,3},{2,0},{3,1},{4,6},{5,7},{6,4},{7,5},{8,10},{9,11},{10,... | collective-permute-start | bytes 786440 | tf_op jit(solution)/shard_map/ppermute | solution.py:9
  256.0 64.4 %collective-permute-start.5 = (f32[32,2048]{1,0:T(8,128)S(1)}, f32[32,2048]{1,0:T(8,128)S(1)}, u32[]{:S(2)}, u32[]{:S(2)}) collective-permute-start(f32[32,2048]{1,0:T(8,128)S(1)} %add_select_fusion), channel_id=1, source_target_pairs={{0,4},{1,5},{2,6},{3,7},{4,0},{5,1},{6,2},{7,3},{8,12},{9,13},{10,... | collective-permute-start | bytes 786440 | tf_op jit(solution)/shard_map/ppermute | solution.py:9
Sparse Core Ops, SparseCore 0:
  35.4 70.1 all-gather.1
  108.2 128.8 reduce-scatter.4
  241.2 77.5 reduce-scatter.2
